TPU v7x, 32 devices: a whole 2x2x4 slice. The times are simulated.
32 devices in a mesh: frame: 4 (over x, core), within: 8 (over z, y).
Axes of the slice: x: 2, y: 2, z: 4, core: 2. Of those that a mesh axis runs over, the one named last changes fastest.
Arguments:
- queries: bfloat16 [4, 576, 1024], P('frame', 'within'), may hold values from -6 to 6
- keys_in: bfloat16 [4, 576, 1024], P('frame', 'within'), may hold values from -6 to 6
- values_in: bfloat16 [4, 576, 1024], P('frame', 'within'), may hold values from -6 to 6
- grad_out: bfloat16 [4, 576, 1024], P('frame', 'within'), may hold values from -6 to 6
- partners: int32 [4, 2], replicated, may hold values from 0 to 3
- registers: int32 [4], replicated, may hold values from 1 to 144
Outputs:
- grad_queries: bfloat16 [4, 576, 1024], P('frame', 'within')
- grad_keys: bfloat16 [4, 576, 1024], P('frame', 'within')
- grad_values: bfloat16 [4, 576, 1024], P('frame', 'within')
Inputs may be any that keep to these rules, and one draw needn't show every extreme that they name: `partners`: A row may list a group more than once, and may list its own group.
All inputs are finite; a program needn't handle non-finite values.
Results may differ from a plain program's by a relative error of at most 0.012.
Values may be sent and summed in bfloat16 or wider, within the bound.
A program may use at most 128 MiB of HBM per device.

v0:
```python
import jax
import jax.numpy as jnp
from jax import lax
from jax.sharding import PartitionSpec as P

DH = 64


def local(queries, keys_in, values_in, grad_out, partners, registers):
    q_wide, k_wide, v_wide, d_wide = (
        lax.all_to_all(queries, "within", split_axis=2, concat_axis=1, tiled=True),
        lax.all_to_all(keys_in, "within", split_axis=2, concat_axis=1, tiled=True),
        lax.all_to_all(values_in, "within", split_axis=2, concat_axis=1, tiled=True),
        lax.all_to_all(grad_out, "within", split_axis=2, concat_axis=1, tiled=True),
    )
    seq = q_wide.shape[1]
    cols = q_wide.shape[2]
    heads_here = cols // DH
    scale = DH ** (-0.5)

    def split_heads(block):
        return block.reshape(seq, heads_here, DH)

    query3 = split_heads(q_wide[0])
    key3 = split_heads(k_wide[0])
    value3 = split_heads(v_wide[0])
    cotan3 = split_heads(d_wide[0])
    group = lax.axis_index("frame")
    listed = partners[group]
    positions = jnp.arange(seq, dtype=jnp.int32)
    everyone = jnp.ones((seq,), jnp.float32)
    groups = lax.axis_size("frame") * queries.shape[0]

    def patches(other):
        return (positions >= registers[other]).astype(jnp.float32)

    def logits(keys_here, visible):
        raw = (
            jnp.einsum("qhd,khd->hqk", query3, keys_here, preferred_element_type=jnp.float32)
            * scale
        )
        return jnp.where(visible[None, None, :] > 0, raw, -1e30)

    def stats(state, keys_here, values_here, visible, weight):
        old_top, old_total, old_dsum = state
        raw = logits(keys_here, visible)
        top = jnp.max(raw, axis=2)
        expo = jnp.exp(raw - top[:, :, None])
        dprod = jnp.einsum("qhd,khd->hqk", cotan3, values_here, preferred_element_type=jnp.float32)
        total = weight * jnp.sum(expo, axis=2)
        dsum = weight * jnp.sum(expo * dprod, axis=2)
        new_top = jnp.maximum(old_top, top)
        keep_old = jnp.exp(old_top - new_top)
        keep_new = jnp.exp(top - new_top)
        return (
            new_top,
            old_total * keep_old + total * keep_new,
            old_dsum * keep_old + dsum * keep_new,
        )

    def grads(final, keys_here, values_here, visible, weight):
        top, total, delta = final
        raw = logits(keys_here, visible)
        prob = jnp.exp(raw - top[:, :, None]) / total[:, :, None]
        dprod = jnp.einsum("qhd,khd->hqk", cotan3, values_here, preferred_element_type=jnp.float32)
        dscore = prob * (dprod - delta[:, :, None])
        dscore_low = dscore.astype(jnp.bfloat16)
        dq_add = jnp.einsum(
            "hqk,khd->qhd", dscore_low, keys_here, preferred_element_type=jnp.float32
        ) * (scale * weight)
        prob_low = prob.astype(jnp.bfloat16)
        dk_add = jnp.einsum(
            "hqk,qhd->khd", dscore_low, query3, preferred_element_type=jnp.float32
        ) * (scale * weight)
        dv_add = (
            jnp.einsum("hqk,qhd->khd", prob_low, cotan3, preferred_element_type=jnp.float32)
            * weight
        )
        return (dq_add.reshape(seq, cols), dk_add.reshape(seq, cols), dv_add.reshape(seq, cols))

    blank = jnp.zeros((heads_here, seq), jnp.float32)
    state = stats((blank - 1e30, blank, blank), key3, value3, everyone, 1.0)
    keys_all, values_all = (
        lax.all_gather(k_wide, "frame", axis=0, tiled=True),
        lax.all_gather(v_wide, "frame", axis=0, tiled=True),
    )
    for slot in range(listed.shape[0]):
        other = listed[slot]
        state = stats(
            state, split_heads(keys_all[other]), split_heads(values_all[other]), patches(other), 1.0
        )
    top, total, dsum = state
    final = (top, total, dsum / total)
    own_terms = grads(final, key3, value3, everyone, 1.0)
    empty = jnp.zeros((groups, seq, cols), jnp.float32)
    results = (own_terms[0], empty.at[group].add(own_terms[1]), empty.at[group].add(own_terms[2]))
    for slot in range(listed.shape[0]):
        other = listed[slot]
        added = grads(
            final, split_heads(keys_all[other]), split_heads(values_all[other]), patches(other), 1.0
        )
        results = (
            results[0] + added[0],
            results[1].at[other].add(added[1]),
            results[2].at[other].add(added[2]),
        )
    dq_sum = results[0]
    got_keys, got_values = (
        lax.all_to_all(results[1], "frame", split_axis=0, concat_axis=0, tiled=True),
        lax.all_to_all(results[2], "frame", split_axis=0, concat_axis=0, tiled=True),
    )
    dk_mine = jnp.sum(got_keys, axis=0, keepdims=True)
    dv_mine = jnp.sum(got_values, axis=0, keepdims=True)
    dq_low = dq_sum.astype(jnp.bfloat16)[None]
    dk_low = dk_mine.astype(jnp.bfloat16)
    dv_low = dv_mine.astype(jnp.bfloat16)
    return (
        lax.all_to_all(dq_low, "within", split_axis=1, concat_axis=2, tiled=True),
        lax.all_to_all(dk_low, "within", split_axis=1, concat_axis=2, tiled=True),
        lax.all_to_all(dv_low, "within", split_axis=1, concat_axis=2, tiled=True),
    )


def solution(mesh):
    placed = (
        P("frame", "within", None),
        P("frame", "within", None),
        P("frame", "within", None),
        P("frame", "within", None),
        P(),
        P(),
    )
    return jax.shard_map(
        local,
        mesh=mesh,
        in_specs=placed,
        out_specs=(
            P("frame", "within", None),
            P("frame", "within", None),
            P("frame", "within", None),
        ),
        check_vma=False,
    )
```

profile of v0, /device:TPU:0, one launch (start us, length us, event | category | flops | bytes accessed | tf_op | source)
XLA Modules:
  0.0 192.7 jit_solution(5798555888546599513)
XLA Ops:
  0.7 1.3 copy.110
  2.5 2.4 %reduce.31 = bf16[1024,72]{1,0:T(8,128)(2,1)S(1)} reduce(bf16[1024,1,72]{2,1,0:T(2,128)(2,1)S(1)} %bitcast.216, bf16[]{:T(256)} %broadcast.248), dimensions={1}, to_apply=%bitcast.168.reduce_sub_computation | reduce | bytes 294914
  4.9 1.2 reshape.379
  6.1 7.3 %all-to-all-start.1 = ((bf16[8,2,4608]{2,1,0:T(2,128)(2,1)}), bf16[8,2,4608]{2,1,0:T(2,128)(2,1)S(1)}, u32[]{:S(2)}, u32[]{:S(2)}) async-start(bf16[8,2,4608]{2,1,0:T(2,128)(2,1)} %reshape.379), calls=%async_computation.1 | async-start | bytes 294912 | tf_op jit(solution)/shard_map/all_to_all | solution.py:12
  16.7 1.2 copy.120
  18.0 2.4 %reduce.30 = bf16[1024,72]{1,0:T(8,128)(2,1)S(1)} reduce(bf16[1024,1,72]{2,1,0:T(2,128)(2,1)S(1)} %bitcast.221, bf16[]{:T(256)} %broadcast.248), dimensions={1}, to_apply=%bitcast.170.reduce_sub_computation | reduce | bytes 294914
  20.4 1.2 reshape.381
  24.3 6.0 %all-to-all-start.3 = ((bf16[8,2,4608]{2,1,0:T(2,128)(2,1)}), bf16[8,2,4608]{2,1,0:T(2,128)(2,1)S(1)}, u32[]{:S(2)}, u32[]{:S(2)}) async-start(bf16[8,2,4608]{2,1,0:T(2,128)(2,1)} %reshape.381), calls=%async_computation.3 | async-start | bytes 294912 | tf_op jit(solution)/shard_map/all_to_all | solution.py:13
  30.3 1.3 convert_compare_fusion
  32.1 2.4 %reduce.32 = bf16[1024,72]{1,0:T(8,128)(2,1)S(1)} reduce(bf16[1024,1,72]{2,1,0:T(2,128)(2,1)S(1)} %bitcast.222, bf16[]{:T(256)} %broadcast.248), dimensions={1}, to_apply=%bitcast.174.reduce_sub_computation | reduce | bytes 294914
  34.5 1.2 reshape.385
  36.0 2.4 %reduce.33 = bf16[1024,72]{1,0:T(8,128)(2,1)S(1)} reduce(bf16[1024,1,72]{2,1,0:T(2,128)(2,1)S(1)} %bitcast.223, bf16[]{:T(256)} %broadcast.248), dimensions={1}, to_apply=%bitcast.172.reduce_sub_computation | reduce | bytes 294914
  40.9 6.0 %all-to-all-start = ((bf16[8,2,4608]{2,1,0:T(2,128)(2,1)}), bf16[8,2,4608]{2,1,0:T(2,128)(2,1)S(1)}, u32[]{:S(2)}, u32[]{:S(2)}) async-start(bf16[8,2,4608]{2,1,0:T(2,128)(2,1)} %reshape.385), calls=%async_computation | async-start | bytes 294912 | tf_op jit(solution)/shard_map/all_to_all | solution.py:11
  48.2 7.5 %all_gather.6 = bf16[4,576,128]{2,1,0:T(8,128)(2,1)S(1)} all-gather(bf16[1,576,128]{2,1,0:T(8,128)(2,1)S(1)} %bitcast.249), channel_id=1, replica_groups=mesh['frame'=4,'within'=8] {'frame'}, dimensions={0}, use_global_device_ids=true | all-gather | bytes 737280 | tf_op jit(solution)/shard_map/all_gather | solution.py:84
  55.8 7.6 %all_gather.7 = bf16[4,576,128]{2,1,0:T(8,128)(2,1)S(1)} all-gather(bf16[1,576,128]{2,1,0:T(8,128)(2,1)S(1)} %bitcast.254), channel_id=1, replica_groups=mesh['frame'=4,'within'=8] {'frame'}, dimensions={0}, use_global_device_ids=true | all-gather | bytes 737280 | tf_op jit(solution)/shard_map/all_gather | solution.py:85
  63.4 6.0 %all-to-all-start.2 = ((bf16[8,2,4608]{2,1,0:T(2,128)(2,1)}), bf16[8,2,4608]{2,1,0:T(2,128)(2,1)S(1)}, u32[]{:S(2)}, u32[]{:S(2)}) async-start(bf16[8,2,4608]{2,1,0:T(2,128)(2,1)} %reshape.383), calls=%async_computation.2 | async-start | bytes 294912 | tf_op jit(solution)/shard_map/all_to_all | solution.py:14
  73.3 3.9 %all-to-all-done.2 = bf16[8,2,4608]{2,1,0:T(2,128)(2,1)S(1)} async-done(((bf16[8,2,4608]{2,1,0:T(2,128)(2,1)}), bf16[8,2,4608]{2,1,0:T(2,128)(2,1)S(1)}, u32[]{:S(2)}, u32[]{:S(2)}) %all-to-all-start.2) | async-done | bytes 147488 | tf_op jit(solution)/shard_map/all_to_all | solution.py:14
  81.6 1.5 multiply_reduce_fusion.1
  83.1 1.6 bitcast_reduce_fusion
  85.5 2.8 %fusion.14 = (f32[2,576]{1,0:T(2,128)S(1)}, f32[2,576]{1,0:T(2,128)S(1)}, f32[2,576,576]{2,1,0:T(8,128)}) fusion(f32[2,576,576]{2,1,0:T(8,128)S(1)} %get-tuple-element.99, f32[2,576]{1,0:T(2,128)S(1)} %get-tuple-element.98, pred[576]{0:T(1024)(128)(4,1)S(1)} %get-tuple-element.109, bf16[576,2,64]{0,2,1:T(8,128)(2,1)S(1)} %bitcast.238, ...), kind=kOutput, calls=%fused_computation.30 | convolution fusion | flops 88913664 | bytes 5617728 | tf_op jit(solution)/shard_map/qhd,khd->hqk/dot_general | solution.py:49
  88.3 2.8 %fusion.13 = (f32[2,576]{1,0:T(2,128)S(1)}, f32[2,576]{1,0:T(2,128)S(1)}, f32[2,576,576]{2,1,0:T(8,128)}) fusion(f32[2,576,576]{2,1,0:T(8,128)S(1)} %get-tuple-element.102, f32[2,576]{1,0:T(2,128)S(1)} %get-tuple-element.101, pred[576]{0:T(1024)(128)(4,1)S(1)} %get-tuple-element.110, bf16[576,2,64]{0,2,1:T(8,128)(2,1)S(1)} %bitcast.239, ...), kind=kOutput, calls=%fused_computation.29 | convolution fusion | flops 88913664 | bytes 5617728 | tf_op jit(solution)/shard_map/qhd,khd->hqk/dot_general | solution.py:49
  91.0 2.5 %fusion.12 = (f32[2,576]{1,0:T(2,128)S(1)}, f32[2,576]{1,0:T(2,128)S(1)}, f32[2,576,576]{1,2,0:T(8,128)}) fusion(f32[2,576,576]{1,2,0:T(8,128)S(1)} %get-tuple-element.105, f32[2,576]{1,0:T(2,128)S(1)} %get-tuple-element.104, bf16[576,2,64]{0,2,1:T(8,128)(2,1)S(1)} %reshape_squeeze.32, bf16[576,2,64]{0,2,1:T(8,128)(2,1)S(1)} %copy-done.14), kind=kOutput, calls=%fused_computation.28 | convolution fusion | flops 88250112 | bytes 5617152 | tf_op jit(solution)/shard_map/qhd,khd->hqk/dot_general | solution.py:65
  93.6 1.7 fusion.15
  95.3 1.7 fusion.17
  97.0 1.8 copy.145
  98.8 1.8 copy.143
  100.6 2.0 %fusion.27 = f32[2,576,64]{1,2,0:T(8,128)} fusion(bf16[576,2,64]{0,2,1:T(8,128)(2,1)S(1)} %reshape_squeeze.32, f32[2,576,576]{1,2,0:T(8,128)S(1)} %get-tuple-element.105, f32[2,576]{1,0:T(2,128)S(1)} %get-tuple-element.87, f32[2,576]{1,0:T(2,128)S(1)} %get-tuple-element.92, pred[]{:T(512)} %get-tuple-element.95), kind=kOutput, calls=%fused_computation.50 | convolution fusion | flops 87662592 | bytes 3105793 | tf_op jit(solution)/shard_map/hqk,qhd->khd/dot_general | solution.py:76
  102.7 1.8 copy.141
  104.5 7.0 %fusion.5 = (bf16[2,576,576]{1,2,0:T(8,128)(2,1)S(1)}, bf16[2,576,576]{1,2,0:T(8,128)(2,1)S(1)}, bf16[2,576,576]{1,2,0:T(8,128)(2,1)S(1)}) fusion(f32[2,576,576]{2,1,0:T(8,128)} %get-tuple-element.103, f32[2,576]{1,0:T(2,128)S(1)} %get-tuple-element.88, f32[2,576]{1,0:T(2,128)S(1)} %get-tuple-element.87, f32[2,576]{1,0:T(2,128)S(1)} %get-tuple-element.92, ...), kind=kLoop, calls=%fused_computation.9 | loop fusion | flops 13271040 | bytes 19921536 | tf_op jit(solution)/shard_map/convert_element_type | solution.py:67
  113.8 1.6 reduce.34
  116.1 4.0 %all-to-all-start.4 = ((bf16[8,2,4608]{2,1,0:T(2,128)(2,1)}), bf16[8,2,4608]{2,1,0:T(2,128)(2,1)}, u32[]{:S(2)}, u32[]{:S(2)}) async-start(bf16[8,2,4608]{2,1,0:T(2,128)(2,1)} %reshape.387), calls=%async_computation.4 | async-start | bytes 294912 | tf_op jit(solution)/shard_map/all_to_all | solution.py:118
  121.9 2.5 %fusion.33 = f32[4,576,128]{2,1,0:T(8,128)} fusion(f32[4,576,128]{2,1,0:T(8,128)} %constant_dynamic-update-slice_fusion, s32[]{:T(128)} %select_n.49, f32[1,576,128]{2,1,0:T(8,128)} %copy.143, pred[]{:T(512)} %get-tuple-element.82), kind=kLoop, calls=%fused_computation.58 | loop fusion | flops 147456 | bytes 885760 | tf_op jit(solution)/shard_map/scatter-add | solution.py:105
  124.5 2.4 %fusion.34 = f32[4,576,128]{2,1,0:T(8,128)} fusion(f32[4,576,128]{2,1,0:T(8,128)} %fusion.33, s32[]{:T(128)} %select_n.52, f32[1,576,128]{2,1,0:T(8,128)S(1)} %copy-done.12, pred[]{:T(512)} %get-tuple-element.81), kind=kLoop, calls=%fused_computation.59 | loop fusion | flops 147456 | bytes 885760 | tf_op jit(solution)/shard_map/scatter-add | solution.py:105
  128.0 4.4 %all-to-all-start.7 = ((f32[4,576,128]{2,1,0:T(8,128)}), f32[4,576,128]{2,1,0:T(8,128)}, u32[]{:S(2)}, u32[]{:S(2)}) async-start(f32[4,576,128]{2,1,0:T(8,128)} %fusion.34), calls=%async_computation.7 | async-start | bytes 2359296 | tf_op jit(solution)/shard_map/all_to_all | solution.py:110
  132.5 1.3 convolution_multiply_fusion.2
  137.6 2.3 %fusion.31 = f32[4,576,128]{2,1,0:T(8,128)} fusion(f32[4,576,128]{2,1,0:T(8,128)} %constant_dynamic-update-slice_fusion.1, s32[]{:T(128)} %select_n.49, f32[1,576,128]{2,1,0:T(8,128)S(1)} %copy.134, pred[]{:T(512)} %get-tuple-element.82), kind=kLoop, calls=%fused_computation.56 | loop fusion | flops 147456 | bytes 885760 | tf_op jit(solution)/shard_map/scatter-add | solution.py:104
  139.9 2.4 %fusion.32 = f32[4,576,128]{2,1,0:T(8,128)} fusion(f32[4,576,128]{2,1,0:T(8,128)} %fusion.31, s32[]{:T(128)} %select_n.52, f32[1,576,128]{2,1,0:T(8,128)S(1)} %copy.136, pred[]{:T(512)} %get-tuple-element.81), kind=kLoop, calls=%fused_computation.57 | loop fusion | flops 147456 | bytes 885760 | tf_op jit(solution)/shard_map/scatter-add | solution.py:104
  142.3 6.1 %all-to-all-done.7 = f32[4,576,128]{2,1,0:T(8,128)} async-done(((f32[4,576,128]{2,1,0:T(8,128)}), f32[4,576,128]{2,1,0:T(8,128)}, u32[]{:S(2)}, u32[]{:S(2)}) %all-to-all-start.7) | async-done | bytes 1179680 | tf_op jit(solution)/shard_map/all_to_all | solution.py:110
  148.3 3.5 %all-to-all-start.5 = ((f32[4,576,128]{2,1,0:T(8,128)}), f32[4,576,128]{2,1,0:T(8,128)S(1)}, u32[]{:S(2)}, u32[]{:S(2)}) async-start(f32[4,576,128]{2,1,0:T(8,128)} %fusion.32), calls=%async_computation.5 | async-start | bytes 2359296 | tf_op jit(solution)/shard_map/all_to_all | solution.py:109
  151.9 1.3 reduce_sum.79
  153.6 1.5 reduce.36
  155.8 11.9 %all-to-all-done.5 = f32[4,576,128]{2,1,0:T(8,128)S(1)} async-done(((f32[4,576,128]{2,1,0:T(8,128)}), f32[4,576,128]{2,1,0:T(8,128)S(1)}, u32[]{:S(2)}, u32[]{:S(2)}) %all-to-all-start.5) | async-done | bytes 1179680 | tf_op jit(solution)/shard_map/all_to_all | solution.py:109
  167.7 5.9 %all-to-all-start.8 = ((bf16[8,2,4608]{2,1,0:T(2,128)(2,1)}), bf16[8,2,4608]{2,1,0:T(2,128)(2,1)S(1)}, u32[]{:S(2)}, u32[]{:S(2)}) async-start(bf16[8,2,4608]{2,1,0:T(2,128)(2,1)} %reshape.391), calls=%async_computation.8 | async-start | bytes 294912 | tf_op jit(solution)/shard_map/all_to_all | solution.py:120
  174.0 1.5 reduce.35
  176.3 4.8 %all-to-all-done.8 = bf16[8,2,4608]{2,1,0:T(2,128)(2,1)S(1)} async-done(((bf16[8,2,4608]{2,1,0:T(2,128)(2,1)}), bf16[8,2,4608]{2,1,0:T(2,128)(2,1)S(1)}, u32[]{:S(2)}, u32[]{:S(2)}) %all-to-all-start.8) | async-done | bytes 147488 | tf_op jit(solution)/shard_map/all_to_all | solution.py:120
  181.0 3.4 %all-to-all-start.6 = ((bf16[8,2,4608]{2,1,0:T(2,128)(2,1)}), bf16[8,2,4608]{2,1,0:T(2,128)(2,1)S(1)}, u32[]{:S(2)}, u32[]{:S(2)}) async-start(bf16[8,2,4608]{2,1,0:T(2,128)(2,1)} %reshape.389), calls=%async_computation.6 | async-start | bytes 294912 | tf_op jit(solution)/shard_map/all_to_all | solution.py:119
  184.4 1.4 reshape.388
  187.4 4.4 %all-to-all-done.6 = bf16[8,2,4608]{2,1,0:T(2,128)(2,1)S(1)} async-done(((bf16[8,2,4608]{2,1,0:T(2,128)(2,1)}), bf16[8,2,4608]{2,1,0:T(2,128)(2,1)S(1)}, u32[]{:S(2)}, u32[]{:S(2)}) %all-to-all-start.6) | async-done | bytes 147488 | tf_op jit(solution)/shard_map/all_to_all | solution.py:119
  (114 shorter events, 30.3 us)
Async XLA Ops:
  0.6 12.7 %copy-start = (s32[4,2]{0,1:T(2,128)S(1)}, s32[4,2]{0,1:T(2,128)}, u32[]{:S(2)}) copy-start(s32[4,2]{0,1:T(2,128)} %param.22) | copy-start | bytes 100
  0.6 22.9 %copy-start.19 = (s32[3]{0:T(128)S(1)}, s32[3]{0:T(128)}, u32[]{:S(2)}) copy-start(s32[3]{0:T(128)} %constant.142.clone.1) | copy-start | bytes 40
  0.7 22.2 %copy-start.18 = (s32[4]{0:T(128)S(1)}, s32[4]{0:T(128)}, u32[]{:S(2)}) copy-start(s32[4]{0:T(128)} %param.23) | copy-start | bytes 52
  0.7 31.0 %copy-start.16 = (bf16[1,72,1024]{2,1,0:T(8,128)(2,1)S(1)}, bf16[1,72,1024]{2,1,0:T(8,128)(2,1)}, u32[]{:S(2)}) copy-start(bf16[1,72,1024]{2,1,0:T(8,128)(2,1)} %param.18) | copy-start | bytes 442372
  2.0 33.7 %copy-start.17 = (bf16[1,72,1024]{2,1,0:T(8,128)(2,1)S(1)}, bf16[1,72,1024]{2,1,0:T(8,128)(2,1)}, u32[]{:S(2)}) copy-start(bf16[1,72,1024]{2,1,0:T(8,128)(2,1)} %param.21) | copy-start | bytes 442372
  6.1 18.3 %all-to-all-start.1 = ((bf16[8,2,4608]{2,1,0:T(2,128)(2,1)}), bf16[8,2,4608]{2,1,0:T(2,128)(2,1)S(1)}, u32[]{:S(2)}, u32[]{:S(2)}) async-start(bf16[8,2,4608]{2,1,0:T(2,128)(2,1)} %reshape.379), calls=%async_computation.1 | async-start | bytes 294912 | tf_op jit(solution)/shard_map/all_to_all | solution.py:12
  24.3 16.6 %all-to-all-start.3 = ((bf16[8,2,4608]{2,1,0:T(2,128)(2,1)}), bf16[8,2,4608]{2,1,0:T(2,128)(2,1)S(1)}, u32[]{:S(2)}, u32[]{:S(2)}) async-start(bf16[8,2,4608]{2,1,0:T(2,128)(2,1)} %reshape.381), calls=%async_computation.3 | async-start | bytes 294912 | tf_op jit(solution)/shard_map/all_to_all | solution.py:13
  40.9 22.5 %all-to-all-start = ((bf16[8,2,4608]{2,1,0:T(2,128)(2,1)}), bf16[8,2,4608]{2,1,0:T(2,128)(2,1)S(1)}, u32[]{:S(2)}, u32[]{:S(2)}) async-start(bf16[8,2,4608]{2,1,0:T(2,128)(2,1)} %reshape.385), calls=%async_computation | async-start | bytes 294912 | tf_op jit(solution)/shard_map/all_to_all | solution.py:11
  63.4 13.7 %all-to-all-start.2 = ((bf16[8,2,4608]{2,1,0:T(2,128)(2,1)}), bf16[8,2,4608]{2,1,0:T(2,128)(2,1)S(1)}, u32[]{:S(2)}, u32[]{:S(2)}) async-start(bf16[8,2,4608]{2,1,0:T(2,128)(2,1)} %reshape.383), calls=%async_computation.2 | async-start | bytes 294912 | tf_op jit(solution)/shard_map/all_to_all | solution.py:14
  83.1 2.4 %copy-start.13 = (bf16[1,576,128]{1,2,0:T(8,128)(2,1)S(1)}, bf16[1,576,128]{1,2,0:T(8,128)(2,1)}, u32[]{:S(2)}) copy-start(bf16[1,576,128]{1,2,0:T(8,128)(2,1)} %copy.125) | copy-start | bytes 442372
  84.8 8.8 %copy-start.1 = (f32[2,576,576]{2,1,0:T(8,128)}, f32[2,576,576]{2,1,0:T(8,128)S(1)}, u32[]{:S(2)}) copy-start(f32[2,576,576]{2,1,0:T(8,128)S(1)} %get-tuple-element.99) | copy-start | bytes 7962628
  85.5 9.8 %copy-start.2 = (f32[2,576,576]{2,1,0:T(8,128)}, f32[2,576,576]{2,1,0:T(8,128)S(1)}, u32[]{:S(2)}) copy-start(f32[2,576,576]{2,1,0:T(8,128)S(1)} %get-tuple-element.102) | copy-start | bytes 7962628
  85.5 2.8 %copy-start.15 = (bf16[1,576,128]{1,2,0:T(8,128)(2,1)S(1)}, bf16[1,576,128]{1,2,0:T(8,128)(2,1)}, u32[]{:S(2)}) copy-start(bf16[1,576,128]{1,2,0:T(8,128)(2,1)} %copy.124) | copy-start | bytes 442372
  88.3 2.8 %copy-start.14 = (bf16[576,2,64]{0,2,1:T(8,128)(2,1)S(1)}, bf16[576,2,64]{0,2,1:T(8,128)(2,1)}, u32[]{:S(2)}) copy-start(bf16[576,2,64]{0,2,1:T(8,128)(2,1)} %reshape_squeeze.33) | copy-start | bytes 442372
  104.5 7.0 %copy-start.10 = (bf16[576,2,64]{0,2,1:T(8,128)(2,1)S(1)}, bf16[576,2,64]{0,2,1:T(8,128)(2,1)}, u32[]{:S(2)}) copy-start(bf16[576,2,64]{0,2,1:T(8,128)(2,1)} %reshape_squeeze.29) | copy-start | bytes 442372
  104.5 7.4 %copy-start.9 = (bf16[1,576,128]{1,2,0:T(8,128)(2,1)S(1)}, bf16[1,576,128]{1,2,0:T(8,128)(2,1)}, u32[]{:S(2)}) copy-start(bf16[1,576,128]{1,2,0:T(8,128)(2,1)} %copy.116) | copy-start | bytes 442372
  111.5 1.2 copy-start.3
  111.5 1.6 copy-start.5
  111.6 2.0 %copy-start.7 = (bf16[2,576,576]{1,2,0:T(8,128)(2,1)}, bf16[2,576,576]{1,2,0:T(8,128)(2,1)S(1)}, u32[]{:S(2)}) copy-start(bf16[2,576,576]{1,2,0:T(8,128)(2,1)S(1)} %get-tuple-element.91) | copy-start | bytes 3981316
  112.4 8.8 %copy-start.11 = (f32[1,576,128]{2,1,0:T(8,128)S(1)}, f32[1,576,128]{2,1,0:T(8,128)}, u32[]{:S(2)}) copy-start(f32[1,576,128]{2,1,0:T(8,128)} %copy.141) | copy-start | bytes 884740
  113.5 10.9 %copy-start.12 = (f32[1,576,128]{2,1,0:T(8,128)S(1)}, f32[1,576,128]{2,1,0:T(8,128)}, u32[]{:S(2)}) copy-start(f32[1,576,128]{2,1,0:T(8,128)} %copy.145) | copy-start | bytes 884740
  113.5 13.3 %copy-start.8 = (bf16[2,576,576]{1,2,0:T(8,128)(2,1)S(1)}, bf16[2,576,576]{1,2,0:T(8,128)(2,1)}, u32[]{:S(2)}) copy-start(bf16[2,576,576]{1,2,0:T(8,128)(2,1)} %copy-done.7) | copy-start | bytes 3981316
  116.1 11.9 %all-to-all-start.4 = ((bf16[8,2,4608]{2,1,0:T(2,128)(2,1)}), bf16[8,2,4608]{2,1,0:T(2,128)(2,1)}, u32[]{:S(2)}, u32[]{:S(2)}) async-start(bf16[8,2,4608]{2,1,0:T(2,128)(2,1)} %reshape.387), calls=%async_computation.4 | async-start | bytes 294912 | tf_op jit(solution)/shard_map/all_to_all | solution.py:118
  121.9 10.5 %copy-start.4 = (bf16[2,576,576]{1,2,0:T(8,128)(2,1)S(1)}, bf16[2,576,576]{1,2,0:T(8,128)(2,1)}, u32[]{:S(2)}) copy-start(bf16[2,576,576]{1,2,0:T(8,128)(2,1)} %copy-done.3) | copy-start | bytes 3981316
  128.0 7.0 %copy-start.6 = (bf16[2,576,576]{1,2,0:T(8,128)(2,1)S(1)}, bf16[2,576,576]{1,2,0:T(8,128)(2,1)}, u32[]{:S(2)}) copy-start(bf16[2,576,576]{1,2,0:T(8,128)(2,1)} %copy-done.5) | copy-start | bytes 3981316
  128.0 20.3 %all-to-all-start.7 = ((f32[4,576,128]{2,1,0:T(8,128)}), f32[4,576,128]{2,1,0:T(8,128)}, u32[]{:S(2)}, u32[]{:S(2)}) async-start(f32[4,576,128]{2,1,0:T(8,128)} %fusion.34), calls=%async_computation.7 | async-start | bytes 2359296 | tf_op jit(solution)/shard_map/all_to_all | solution.py:110
  148.3 19.3 %all-to-all-start.5 = ((f32[4,576,128]{2,1,0:T(8,128)}), f32[4,576,128]{2,1,0:T(8,128)S(1)}, u32[]{:S(2)}, u32[]{:S(2)}) async-start(f32[4,576,128]{2,1,0:T(8,128)} %fusion.32), calls=%async_computation.5 | async-start | bytes 2359296 | tf_op jit(solution)/shard_map/all_to_all | solution.py:109
  167.7 13.4 %all-to-all-start.8 = ((bf16[8,2,4608]{2,1,0:T(2,128)(2,1)}), bf16[8,2,4608]{2,1,0:T(2,128)(2,1)S(1)}, u32[]{:S(2)}, u32[]{:S(2)}) async-start(bf16[8,2,4608]{2,1,0:T(2,128)(2,1)} %reshape.391), calls=%async_computation.8 | async-start | bytes 294912 | tf_op jit(solution)/shard_map/all_to_all | solution.py:120
  181.0 10.8 %all-to-all-start.6 = ((bf16[8,2,4608]{2,1,0:T(2,128)(2,1)}), bf16[8,2,4608]{2,1,0:T(2,128)(2,1)S(1)}, u32[]{:S(2)}, u32[]{:S(2)}) async-start(bf16[8,2,4608]{2,1,0:T(2,128)(2,1)} %reshape.389), calls=%async_computation.6 | async-start | bytes 294912 | tf_op jit(solution)/shard_map/all_to_all | solution.py:119
where the time goes:
time: 194 us; the launch traced here: 193 us
  starting transfers between devices  46.5 us (24%)
  local copies, waits for them, and re-layouts  38.9 us (20%)
  other arithmetic  34.3 us (18%)
  waiting for transfers between devices  31 us (16%)
  matrix products  21.4 us (11%)
  blocking collectives  15.2 us (8%)
  between operations  5.27 us (3%)
    unnamed x68, local copies, waits for them, and re-layouts  17.3 us
    unnamed x7, other arithmetic  14.1 us
    all_to_all x1, waiting for transfers between devices, local(): lax.all_to_all(results[1], 'frame', split_axis=0, concat_axis=0, tiled=True)  11.9 us
    all_gather x1, blocking collectives, local(): lax.all_gather(v_wide, 'frame', axis=0, tiled=True)  7.64 us
    all_gather x1, blocking collectives, local(): lax.all_gather(k_wide, 'frame', axis=0, tiled=True)  7.53 us
    all_to_all x1, starting transfers between devices, local(): lax.all_to_all(keys_in, 'within', split_axis=2, concat_axis=1, tiled=True)  7.31 us
    convert_element_type x1, other arithmetic, grads(): dscore_low = dscore.astype(jnp.bfloat16)  7 us
    another operation x6, local copies, waits for them, and re-layouts  6.93 us
  transfers between devices with their start and end apart: 9, of which 5 were waited for; matrix products, arithmetic and copies ran while one was open for 26% of the time, Pallas kernels for 0%

commit v1 on v0

v1 whole, which is shorter than its diff:
```python
import functools
import math

import jax
import jax.numpy as jnp
import numpy as np
from jax import lax
from jax.experimental import pallas as pl
from jax.experimental.pallas import tpu as pltpu
from jax.sharding import PartitionSpec as P

DH = 64
PAIR = 2 * DH
SPLITS = 3
HIDDEN = -1e30
BF = jnp.bfloat16
F32 = jnp.float32
MESH = pl.DeviceIdType.MESH


def pieces_of(value):
    left, out = float(value), []
    for _ in range(SPLITS):
        part = float(np.asarray(left, dtype=jnp.bfloat16))
        out.append(part)
        left = left - part if abs(value) < 1e20 else 0.0
    return out


def rdot(a, b):
    return lax.dot_general(a, b, (((1,), (1,)), ((), ())), preferred_element_type=F32)


def dot(a, b):
    return jnp.dot(a, b, preferred_element_type=F32)


def kernel(F, W, R, QB, part_ref, reg_ref, q_ref, k_ref, v_ref, d_ref, dq_out, dk_out, dv_out,
           kv_send, qd_send, kv_in, qd_in, kaug, vz, kt, qaug, xraw, qz, doz, sbuf, dpbuf, acc, dqs,
           red_send, red_in, fin_send, fin_in, dq_send, dq_in,
           kv_ss, fw_ss, kv_rs, qd_ss, qd_rs, red_ss, red_rs, fin_ss, fin_rs, dq_ss, dq_rs):
    fs = F // R
    half_f = F // 2
    rows = q_ref.shape[1]
    width = q_ref.shape[2]
    seq = rows * W
    n_slots = part_ref.shape[1]
    scale = DH ** -0.5
    half = dq_send.shape[2]
    nq = R * seq
    f = lax.axis_index("frame")
    w = lax.axis_index("within")
    c = lax.rem(f, fs)
    a0 = lax.div(f, fs)
    sib = f + 1 - 2 * lax.rem(f, 2)
    head = w * R + a0

    barrier = pltpu.get_barrier_semaphore()

    def greet(t, carry):
        ff = lax.rem(f + 2 * lax.div(t, W), F)
        ww = lax.rem(w + lax.rem(t, W), W)
        pl.semaphore_signal(barrier, inc=1, device_id=(ff, ww), device_id_type=MESH)
        return carry

    lax.fori_loop(1, half_f * W, greet, 0)
    for dc in range(1, fs, 2):
        pl.semaphore_signal(barrier, inc=1, device_id=(a0 * fs + lax.rem(c + dc, fs), w), device_id_type=MESH)

    for j in range(width // PAIR):
        cols = slice(j * PAIR, (j + 1) * PAIR)
        for first, second, out in ((k_ref, v_ref, kv_send), (q_ref, d_ref, qd_send)):
            one = first[0, :, cols]
            two = second[0, :, cols]
            out[2 * j] = jnp.concatenate([one[:, :DH], two[:, :DH]], axis=1)
            out[2 * j + 1] = jnp.concatenate([one[:, DH:], two[:, DH:]], axis=1)
    kv_in[f, w] = kv_send[head]
    qd_in[a0, w] = qd_send[head]

    pl.semaphore_wait(barrier, half_f * W - 1 + fs // 2)

    def kv_copy(t):
        ff = lax.rem(f + 2 * lax.div(t, W), F)
        ww = lax.rem(w + lax.rem(t, W), W)
        return pltpu.make_async_remote_copy(
            src_ref=kv_send.at[ww * R + lax.div(ff, fs)], dst_ref=kv_in.at[f, w],
            send_sem=kv_ss.at[t], recv_sem=kv_rs.at[f * W + w],
            device_id=(ff, ww), device_id_type=MESH)

    def forward(t):
        ff = lax.rem(f + F - 2 * lax.div(t, W), F)
        ww = lax.rem(w + W - lax.rem(t, W), W)
        return pltpu.make_async_remote_copy(
            src_ref=kv_in.at[ff, ww], dst_ref=kv_in.at[ff, ww],
            send_sem=fw_ss.at[t], recv_sem=kv_rs.at[ff * W + ww],
            device_id=(sib, w), device_id_type=MESH)

    def from_sibling(t):
        ff = lax.rem(sib + F - 2 * lax.div(t, W), F)
        ww = lax.rem(w + W - lax.rem(t, W), W)
        return pltpu.make_async_remote_copy(
            src_ref=kv_in.at[ff, ww], dst_ref=kv_in.at[ff, ww],
            send_sem=fw_ss.at[t], recv_sem=kv_rs.at[ff * W + ww],
            device_id=(sib, w), device_id_type=MESH)

    def peer(t):
        return lax.rem(a0 + lax.div(t, W), R), lax.rem(w + lax.rem(t, W), W)

    def source(t):
        return lax.rem(a0 + R - lax.div(t, W), R), lax.rem(w + W - lax.rem(t, W), W)

    def qd_copy(t):
        aa, ww = peer(t)
        return pltpu.make_async_remote_copy(
            src_ref=qd_send.at[ww * R + aa], dst_ref=qd_in.at[a0, w],
            send_sem=qd_ss.at[t], recv_sem=qd_rs.at[a0 * W + w],
            device_id=(aa * fs + c, ww), device_id_type=MESH)

    def qd_arrival(t):
        aa, ww = source(t)
        return pltpu.make_async_remote_copy(
            src_ref=qd_in.at[aa, ww], dst_ref=qd_in.at[aa, ww],
            send_sem=qd_ss.at[t], recv_sem=qd_rs.at[aa * W + ww],
            device_id=(aa * fs + c, ww), device_id_type=MESH)

    def each(lo, hi, do):
        def step(t, carry):
            do(t)
            return carry
        lax.fori_loop(lo, hi, step, 0)

    forward(0).start()
    each(1, half_f * W, lambda t: kv_copy(t).start())
    each(1, R * W, lambda t: qd_copy(t).start())

    acc[...] = jnp.zeros_like(acc)

    def relay(t):
        move = forward(t)
        move.wait_recv()
        move.start()

    each(1, half_f * W, relay)
    each(0, half_f * W, lambda t: from_sibling(t).wait_recv())

    lane = lax.broadcasted_iota(jnp.int32, (seq, PAIR), 1)
    row = lax.broadcasted_iota(jnp.int32, (seq, PAIR), 0)
    lane1 = lax.broadcasted_iota(jnp.int32, (1, PAIR), 1)
    table = [pieces_of(HIDDEN)] + [pieces_of(math.log(n)) for n in range(1, n_slots + 2)]

    def prepare_keys(p):
        both = kv_in[p].astype(F32).reshape(seq, PAIR)
        seen = jnp.zeros((1, PAIR), F32)
        unseen = jnp.zeros((1, PAIR), F32)
        for gi in range(R):
            g = c + fs * gi
            own = jnp.where(p == g, 1, 0)
            count = own
            for slot in range(n_slots):
                count = count + jnp.where(part_ref[g, slot] == p, 1, 0)
            for e in range(SPLITS):
                here = lane1 == DH + SPLITS * gi + e
                for n in range(n_slots + 2):
                    if n < 2:
                        unseen = jnp.where(here & (own == n), table[n][e], unseen)
                    seen = jnp.where(here & (count == n), table[n][e], seen)
        extra = jnp.where(row >= reg_ref[p], seen, unseen)
        kaug[p] = jnp.where(lane < DH, both, extra).astype(BF)
        vz[p] = jnp.where(lane >= DH, both, 0.0).astype(BF)
        kt[p] = (both * scale).T[:DH].astype(BF)

    each(0, F, prepare_keys)
    each(1, R * W, lambda t: qd_arrival(t).wait_recv())

    for gi in range(R):
        both = qd_in[gi].astype(F32).reshape(seq, PAIR)
        at = slice(gi * seq, (gi + 1) * seq)
        mark = jnp.where((lane >= DH + SPLITS * gi) & (lane < DH + SPLITS * (gi + 1)), 1.0, 0.0)
        scaled = both * scale
        qaug[at] = jnp.where(lane < DH, scaled, mark).astype(BF)
        xraw[at] = both.astype(BF)
        qz[at] = jnp.where(lane < DH, scaled, 0.0).astype(BF)
        doz[at] = jnp.where(lane >= DH, both, 0.0).astype(BF)

    def block(i):
        at = pl.ds(pl.multiple_of(i * QB, QB), QB)

        def scores(p, top):
            raw = rdot(kaug[p], qaug[at])
            sbuf[p] = raw
            return jnp.maximum(top, jnp.max(raw, axis=0, keepdims=True))

        top = lax.fori_loop(0, F, scores, jnp.full((1, QB), -3e38, F32))

        def sums(p, state):
            total, dsum = state
            expo = jnp.exp(sbuf[p] - top)
            dprod = rdot(vz[p], xraw[at])
            sbuf[p] = expo
            dpbuf[p] = dprod
            return (total + jnp.sum(expo, axis=0, keepdims=True),
                    dsum + jnp.sum(expo * dprod, axis=0, keepdims=True))

        blank = jnp.zeros((1, QB), F32)
        total, dsum = lax.fori_loop(0, F, sums, (blank, blank))
        inv = 1.0 / total
        delta = dsum * inv

        def grads(p, dq):
            prob = sbuf[p] * inv
            dscore = (prob * (dpbuf[p] - delta)).astype(BF)
            acc[p] += dot(dscore, qz[at]) + dot(prob.astype(BF), doz[at])
            return dq + dot(kt[p], dscore)

        dq = lax.fori_loop(0, F, grads, jnp.zeros((DH, QB), F32))
        dqs[at] = jnp.concatenate([dq, jnp.zeros((DH, QB), F32)], axis=0).T

    each(0, nq // QB, block)

    def red_copy(dc, gi):
        cp = lax.rem(c + dc, fs)
        return pltpu.make_async_remote_copy(
            src_ref=red_send.at[dc - 1, gi], dst_ref=red_in.at[dc - 1, gi],
            send_sem=red_ss.at[(dc - 1) * R + gi], recv_sem=red_rs.at[(dc - 1) * R + gi],
            device_id=(a0 * fs + cp, w), device_id_type=MESH)

    for dc in range(1, fs):
        cp = lax.rem(c + dc, fs)
        for gi in range(R):
            red_send[dc - 1, gi] = acc[cp + fs * gi].reshape(W, rows, PAIR).astype(BF)
            red_copy(dc, gi).start()

    def dq_copy(t):
        aa, ww = peer(t)
        return pltpu.make_async_remote_copy(
            src_ref=dq_send.at[aa, ww], dst_ref=dq_in.at[head],
            send_sem=dq_ss.at[t], recv_sem=dq_rs.at[head],
            device_id=(aa * fs + c, ww), device_id_type=MESH)

    def dq_arrival(t):
        aa, ww = source(t)
        return pltpu.make_async_remote_copy(
            src_ref=dq_in.at[ww * R + aa], dst_ref=dq_in.at[ww * R + aa],
            send_sem=dq_ss.at[t], recv_sem=dq_rs.at[ww * R + aa],
            device_id=(aa * fs + c, ww), device_id_type=MESH)

    def fin_copy(t):
        aa, ww = peer(t)
        return pltpu.make_async_remote_copy(
            src_ref=fin_send.at[aa, ww], dst_ref=fin_in.at[head],
            send_sem=fin_ss.at[t], recv_sem=fin_rs.at[head],
            device_id=(aa * fs + c, ww), device_id_type=MESH)

    def fin_arrival(t):
        aa, ww = source(t)
        return pltpu.make_async_remote_copy(
            src_ref=fin_in.at[ww * R + aa], dst_ref=fin_in.at[ww * R + aa],
            send_sem=fin_ss.at[t], recv_sem=fin_rs.at[ww * R + aa],
            device_id=(aa * fs + c, ww), device_id_type=MESH)

    for gi in range(R):
        for ww in range(W):
            base = gi * seq + ww * rows
            dq_send[gi, ww] = jnp.concatenate(
                [dqs[base:base + half, :DH], dqs[base + rows - half:base + rows, :DH]], axis=1).astype(BF)
    dq_in[head] = dq_send[a0, w]
    each(1, R * W, lambda t: dq_copy(t).start())

    for gi in range(R):
        whole = acc[c + fs * gi].reshape(W, rows, PAIR)
        for dc in range(1, fs):
            red_copy(dc, gi).wait_recv()
            whole = whole + red_in[dc - 1, gi].astype(F32)
        fin_send[gi] = whole.astype(BF)
    fin_in[head] = fin_send[a0, w]
    each(1, R * W, lambda t: fin_copy(t).start())

    each(1, R * W, lambda t: dq_arrival(t).wait_recv())
    for j in range(width // PAIR):
        cols = slice(j * PAIR, (j + 1) * PAIR)
        sides = []
        for h in (2 * j, 2 * j + 1):
            got = dq_in[h].astype(F32)
            sides.append(jnp.concatenate([got[:, :DH], got[2 * half - rows:, DH:]], axis=0))
        dq_out[0, :, cols] = jnp.concatenate(sides, axis=1).astype(BF)

    each(1, R * W, lambda t: fin_arrival(t).wait_recv())
    for j in range(width // PAIR):
        cols = slice(j * PAIR, (j + 1) * PAIR)
        one, two = fin_in[2 * j], fin_in[2 * j + 1]
        dk_out[0, :, cols] = jnp.concatenate([one[:, :DH], two[:, :DH]], axis=1)
        dv_out[0, :, cols] = jnp.concatenate([one[:, DH:], two[:, DH:]], axis=1)

    each(1, half_f * W, lambda t: kv_copy(t).wait_send())
    each(0, half_f * W, lambda t: forward(t).wait_send())
    each(1, R * W, lambda t: qd_copy(t).wait_send())
    each(1, R * W, lambda t: dq_copy(t).wait_send())
    each(1, R * W, lambda t: fin_copy(t).wait_send())
    for dc in range(1, fs):
        for gi in range(R):
            red_copy(dc, gi).wait_send()


def local(F, W, queries, keys_in, values_in, grad_out, partners, registers):
    _, rows, width = queries.shape
    heads = width // DH
    R = heads // W
    fs = F // R
    seq = rows * W
    nq = R * seq
    half = ((rows + 1) // 2 + 7) // 8 * 8
    QB = next(b for b in (384, 256, 128) if nq % b == 0 and F * seq * b * 8 <= 20 * 2 ** 20)
    vm = lambda *shape: pltpu.VMEM(shape, BF)
    vf = lambda *shape: pltpu.VMEM(shape, F32)
    dma = lambda n: pltpu.SemaphoreType.DMA((n,))
    out = jax.ShapeDtypeStruct((1, rows, width), BF)
    return pl.pallas_call(
        functools.partial(kernel, F, W, R, QB),
        out_shape=(out, out, out),
        in_specs=[pl.BlockSpec(memory_space=pltpu.SMEM)] * 2 + [pl.BlockSpec(memory_space=pltpu.VMEM)] * 4,
        out_specs=(pl.BlockSpec(memory_space=pltpu.VMEM),) * 3,
        scratch_shapes=[
            vm(heads, rows, PAIR), vm(heads, rows, PAIR),
            vm(F, W, rows, PAIR), vm(R, W, rows, PAIR),
            vm(F, seq, PAIR), vm(F, seq, PAIR), vm(F, DH, seq),
            vm(nq, PAIR), vm(nq, PAIR), vm(nq, PAIR), vm(nq, PAIR),
            vf(F, seq, QB), vf(F, seq, QB), vf(F, seq, PAIR), vf(nq, PAIR),
            vm(fs - 1, R, W, rows, PAIR), vm(fs - 1, R, W, rows, PAIR),
            vm(R, W, rows, PAIR), vm(heads, rows, PAIR),
            vm(R, W, half, PAIR), vm(heads, half, PAIR),
            dma(F // 2 * W), dma(F // 2 * W), dma(F * W), dma(R * W), dma(R * W),
            dma((fs - 1) * R), dma((fs - 1) * R), dma(R * W), dma(heads), dma(R * W), dma(heads),
        ],
        compiler_params=pltpu.CompilerParams(
            collective_id=0, has_side_effects=True, vmem_limit_bytes=60 * 2 ** 20),
    )(partners, registers, queries, keys_in, values_in, grad_out)


def solution(mesh):
    spec = P("frame", "within", None)
    return jax.shard_map(
        functools.partial(local, mesh.shape["frame"], mesh.shape["within"]),
        mesh=mesh,
        in_specs=(spec, spec, spec, spec, P(), P()),
        out_specs=(spec, spec, spec),
        check_vma=False,
    )
```

time: 194 us -> 56.2 us (0.29)
  Pallas kernels: 0 us -> 50.7 us
  starting transfers between devices: 46.5 us -> 0 us
  local copies, waits for them, and re-layouts: 38.9 us -> 4.58 us
  other arithmetic: 34.3 us -> 0 us
  waiting for transfers between devices: 31 us -> 0 us
  matrix products: 21.4 us -> 0 us
  blocking collectives: 15.2 us -> 0 us
  between operations: 5.27 us -> 0.65 us
    pallas_call x0 -> x1, Pallas kernels: none -> 50.7 us  [local(): pl.pallas_call(functools.partial(kernel, F, W, R, QB), out_shape=(out, ou...]
    all_to_all x9 -> x0, starting transfers between devices: 46.5 us -> none  [the longest x1 7.31 us: local(): lax.all_to_all(keys_in, 'within', split_axis=2, concat_axis=1, tiled=True)]
    all_to_all x9 -> x0, waiting for transfers between devices: 31 us -> none  [the longest x1 11.9 us: local(): lax.all_to_all(results[1], 'frame', split_axis=0, concat_axis=0, tiled=True)]
    dot_general x15 -> x0, matrix products: 21.4 us -> none  [the longest x2 5.52 us: stats(): jnp.einsum('qhd,khd->hqk', cotan3, values_here, preferred_element_type=jn...]
    all_gather x2 -> x0, blocking collectives: 15.2 us -> none  [the longest x1 7.64 us: local(): lax.all_gather(v_wide, 'frame', axis=0, tiled=True)]
    unnamed x7 -> x0, other arithmetic: 14.1 us -> none
    unnamed x68 -> x8, local copies, waits for them, and re-layouts: 17.3 us -> 4.58 us
    scatter-add x4 -> x0, other arithmetic: 9.66 us -> none  [the longest x2 4.92 us: local(): results[2].at[other].add(added[2])]
  transfers between devices with their start and end apart: 9 -> 0, of which waited for: 5 -> 0; matrix products, arithmetic and copies ran while one was open for 26% -> 0% of each run, Pallas kernels for 0% -> 0%
where the time goes in v1:
time: 56.2 us; the launch traced here: 56 us
  Pallas kernels  50.7 us (90%)
  local copies, waits for them, and re-layouts  4.58 us (8%)
  between operations  0.65 us (1%)
    pallas_call x1, Pallas kernels, local(): pl.pallas_call(functools.partial(kernel, F, W, R, QB), out_shape=(out, ou...  50.7 us
    unnamed x8, local copies, waits for them, and re-layouts  4.58 us

profile of v1, /device:TPU:0, one launch (start us, length us, event | category | flops | bytes accessed | tf_op | source)
XLA Modules:
  0.0 56.0 jit_solution(779301756903114159)
XLA Ops:
  0.6 1.3 %copy.9.part_ref = s32[4,2]{1,0:T(4,128)} copy(s32[4,2]{0,1:T(2,128)} %param.10) | data formatting | bytes 64 | tf_op args[4]
  2.0 50.7 %shard_map.85 = (bf16[1,72,1024]{2,1,0:T(8,128)(2,1)}, bf16[1,72,1024]{2,1,0:T(8,128)(2,1)}, bf16[1,72,1024]{2,1,0:T(8,128)(2,1)}) custom-call(s32[4,2]{1,0:T(4,128)} %copy.9.part_ref, s32[4]{0:T(128)} %reg_ref.1, bf16[1,72,1024]{2,1,0:T(8,128)(2,1)} %q_ref.1, bf16[1,72,1024]{2,1,0:T(8,128)(2,1)} %k_ref.1, bf16[1,72,1024]{2,1,0:T(8,128)(2,1)} %v_ref.1, ...), custom_call_target="tpu_custom_call" | custom-call | tf_op jit(solution)/shard_map/pallas_call | solution.py:317
  52.7 0.0 copy-start.1
  52.7 1.6 %copy.13 = bf16[1,72,1024]{2,1,0:T(8,128)(2,1)} copy(bf16[1,72,1024]{2,1,0:T(8,128)(2,1)} %get-tuple-element.6) | data formatting | bytes 294912
  54.3 0.0 copy-done.1
  54.3 0.0 copy-start
  54.3 0.7 %copy.14 = bf16[1,72,1024]{2,1,0:T(8,128)(2,1)} copy(bf16[1,72,1024]{2,1,0:T(8,128)(2,1)S(1)} %copy-done.1) | data formatting | bytes 294912
  55.0 0.3 copy-done
  55.3 0.7 %copy.15 = bf16[1,72,1024]{2,1,0:T(8,128)(2,1)} copy(bf16[1,72,1024]{2,1,0:T(8,128)(2,1)S(1)} %copy-done) | data formatting | bytes 294912
Async XLA Ops:
  52.7 1.6 %copy-start.1 = (bf16[1,72,1024]{2,1,0:T(8,128)(2,1)S(1)}, bf16[1,72,1024]{2,1,0:T(8,128)(2,1)}, u32[]{:S(2)}) copy-start(bf16[1,72,1024]{2,1,0:T(8,128)(2,1)} %get-tuple-element.7) | copy-start | bytes 442372
  54.3 1.0 %copy-start = (bf16[1,72,1024]{2,1,0:T(8,128)(2,1)S(1)}, bf16[1,72,1024]{2,1,0:T(8,128)(2,1)}, u32[]{:S(2)}) copy-start(bf16[1,72,1024]{2,1,0:T(8,128)(2,1)} %get-tuple-element.8) | copy-start | bytes 442372

commit v2 on v1

v2 whole, which is shorter than its diff:
```python
import functools
import math

import jax
import jax.numpy as jnp
import numpy as np
from jax import lax
from jax.experimental import pallas as pl
from jax.experimental.pallas import tpu as pltpu
from jax.sharding import PartitionSpec as P

DH = 64
PAIR = 2 * DH
SPLITS = 3
UNIT = 640
HIDDEN = -1e30
BF = jnp.bfloat16
F32 = jnp.float32
MESH = pl.DeviceIdType.MESH


def pieces_of(value):
    left, out = float(value), []
    for _ in range(SPLITS):
        part = float(np.asarray(left, dtype=jnp.bfloat16))
        out.append(part)
        left = left - part if abs(value) < 1e20 else 0.0
    return out


def rdot(a, b):
    return lax.dot_general(a, b, (((1,), (1,)), ((), ())), preferred_element_type=F32)


def dot(a, b):
    return jnp.dot(a, b, preferred_element_type=F32)


def each(lo, hi, do):
    def step(t, carry):
        do(t)
        return carry
    lax.fori_loop(lo, hi, step, 0)


def kernel(F, W, R, QC, inline, part_ref, reg_ref, q_ref, k_ref, v_ref, d_ref, dq_out, dk_out, dv_out,
           kv_send, qd_send, kv_in, qd_in, kaug, vz, kt, qaug, xraw, qdz, sbuf, dpbuf, acc, dqacc, dqs,
           tops, top_ref, total_ref, dsum_ref,
           red_send, red_in, fin_send, fin_in, dq_send, dq_in,
           kv_ss, fw_ss, kv_rs, qd_ss, qd_rs, red_ss, red_rs, fin_ss, fin_rs, dq_ss, dq_rs):
    fs = F // R
    hf = F // 2
    rows = q_ref.shape[1]
    width = q_ref.shape[2]
    seq = rows * W
    n_slots = part_ref.shape[0]
    scale = DH ** -0.5
    half = dq_send.shape[2]
    nq = R * seq
    n_chunks = nq // QC
    n_units, per = acc.shape[0], acc.shape[1]
    unit = per * F * rows
    f = lax.axis_index("frame")
    w = lax.axis_index("within")
    c = lax.rem(f, fs)
    a0 = lax.div(f, fs)
    sib = f + 1 - 2 * lax.rem(f, 2)
    head = w * R + a0

    barrier = pltpu.get_barrier_semaphore()

    def ahead(dw):
        return lax.rem(w + dw, W)

    def behind(dw):
        return lax.rem(w + W - dw, W)

    def greet(t):
        pl.semaphore_signal(barrier, inc=1, device_id=(lax.rem(f + 2 * lax.rem(t, hf), F), ahead(lax.div(t, hf))),
                            device_id_type=MESH)

    each(1, hf * W, greet)
    for dc in range(1, fs, 2):
        pl.semaphore_signal(barrier, inc=1, device_id=(a0 * fs + lax.rem(c + dc, fs), w), device_id_type=MESH)

    for first, second, out in ((q_ref, d_ref, qd_send), (k_ref, v_ref, kv_send)):
        for j in range(width // PAIR):
            cols = slice(j * PAIR, (j + 1) * PAIR)
            one = first[0, :, cols]
            two = second[0, :, cols]
            out[2 * j] = jnp.concatenate([one[:, :DH], two[:, :DH]], axis=1)
            out[2 * j + 1] = jnp.concatenate([one[:, DH:], two[:, DH:]], axis=1)
    kv_in[f, w] = kv_send[head]
    qd_in[a0, w] = qd_send[head]

    pl.semaphore_wait(barrier, hf * W - 1 + fs // 2)

    def kv_copy(t):
        ff = lax.rem(f + 2 * lax.rem(t, hf), F)
        ww = ahead(lax.div(t, hf))
        return pltpu.make_async_remote_copy(
            src_ref=kv_send.at[ww * R + lax.div(ff, fs)], dst_ref=kv_in.at[f, w],
            send_sem=kv_ss.at[t], recv_sem=kv_rs.at[f * W + w],
            device_id=(ff, ww), device_id_type=MESH)

    def pass_on(origin, t):
        ff = lax.rem(origin + F - 2 * lax.rem(t, hf), F)
        ww = behind(lax.div(t, hf))
        return pltpu.make_async_remote_copy(
            src_ref=kv_in.at[ff, ww], dst_ref=kv_in.at[ff, ww],
            send_sem=fw_ss.at[t], recv_sem=kv_rs.at[ff * W + ww],
            device_id=(sib, w), device_id_type=MESH)

    def qd_copy(t):
        aa, ww = lax.rem(a0 + lax.rem(t, R), R), ahead(lax.div(t, R))
        return pltpu.make_async_remote_copy(
            src_ref=qd_send.at[ww * R + aa], dst_ref=qd_in.at[a0, w],
            send_sem=qd_ss.at[t], recv_sem=qd_rs.at[a0 * W + w],
            device_id=(aa * fs + c, ww), device_id_type=MESH)

    def arrival(t, buffer, send, recv, index, source):
        return pltpu.make_async_remote_copy(
            src_ref=buffer.at[index], dst_ref=buffer.at[index], send_sem=send.at[t], recv_sem=recv,
            device_id=source, device_id_type=MESH)

    def qd_arrival(t):
        aa, ww = lax.rem(a0 + R - lax.rem(t, R), R), behind(lax.div(t, R))
        return arrival(t, qd_in, qd_ss, qd_rs.at[aa * W + ww], (aa, ww), (aa * fs + c, ww))

    def head_arrival(t, buffer, send, recv):
        aa, ww = lax.rem(a0 + R - lax.rem(t, R), R), ahead(lax.div(t, R))
        return arrival(t, buffer, send, recv.at[ww * R + aa], (ww * R + aa,), (aa * fs + c, ww))

    each(1, R * W, lambda t: qd_copy(t).start())
    pass_on(f, 0).start()
    each(1, hf * W, lambda t: kv_copy(t).start())

    acc[...] = jnp.zeros_like(acc)
    dqacc[...] = jnp.zeros_like(dqacc)

    def relay(t):
        move = pass_on(f, t)
        move.wait_recv()
        move.start()

    lane1 = lax.broadcasted_iota(jnp.int32, (1, PAIR), 1)
    table = [pieces_of(HIDDEN)] + [pieces_of(math.log(n)) for n in range(1, n_slots + 2)]
    marks = []
    for p in range(F):
        seen = jnp.zeros((1, PAIR), F32)
        unseen = jnp.zeros((1, PAIR), F32)
        for gi in range(R):
            g = c + fs * gi
            own = jnp.where(p == g, 1, 0)
            count = own
            for slot in range(n_slots):
                count = count + jnp.where(part_ref[slot, g] == p, 1, 0)
            for e in range(SPLITS):
                here = lane1 == DH + SPLITS * gi + e
                for n in range(n_slots + 2):
                    if n < 2:
                        unseen = jnp.where(here & (own == n), table[n][e], unseen)
                    seen = jnp.where(here & (count == n), table[n][e], seen)
        marks.append((seen, unseen))

    lane = lax.broadcasted_iota(jnp.int32, (rows, PAIR), 1)
    row = lax.broadcasted_iota(jnp.int32, (rows, PAIR), 0)

    def prepare(u):
        aug, raw = [], []
        for d in range(per):
            ww = behind(u * per + d)
            for p in range(F):
                both = kv_in[p, ww].astype(F32)
                extra = jnp.where(row + ww * rows >= reg_ref[p], marks[p][0], marks[p][1])
                raw.append(both)
                aug.append(jnp.where(lane < DH, both, extra))
        raw = jnp.concatenate(raw, axis=0)
        keep = lax.broadcasted_iota(jnp.int32, (unit, PAIR), 1) >= DH
        kaug[u] = jnp.concatenate(aug, axis=0).astype(BF)
        vz[u] = jnp.where(keep, raw, 0.0).astype(BF)
        kt[u] = (raw * scale).T[:DH].astype(BF)

    def direct(u):
        each(max(u * per * hf, 1), (u + 1) * per * hf, relay)

    def settle(u):
        each(u * per * hf, (u + 1) * per * hf, lambda t: pass_on(sib, t).wait_recv())
        prepare(u)

    def rows_of(i):
        return pl.ds(pl.multiple_of(i * QC, QC), QC)

    def begin(b):
        top_ref[b] = jnp.full_like(top_ref[b], -3e38)
        total_ref[b] = jnp.zeros_like(total_ref[b])
        dsum_ref[b] = jnp.zeros_like(dsum_ref[b])

    def forth(u, i, b):
        at = rows_of(i)
        raw = rdot(kaug[u], qaug[at])
        old = top_ref[b]
        top = jnp.maximum(old, jnp.max(raw, axis=0, keepdims=True))
        keep = jnp.exp(old - top)
        expo = jnp.exp(raw - top)
        dprod = rdot(vz[u], xraw[at])
        sbuf[u, b] = expo
        dpbuf[u, b] = dprod
        tops[u, b] = top
        top_ref[b] = top
        total_ref[b] = total_ref[b] * keep + jnp.sum(expo, axis=0, keepdims=True)
        dsum_ref[b] = dsum_ref[b] * keep + jnp.sum(expo * dprod, axis=0, keepdims=True)

    def back(u, i, b):
        inv = 1.0 / total_ref[b]
        factor = jnp.exp(tops[u, b] - top_ref[b]) * inv
        prob = sbuf[u, b] * factor
        dscore = (prob * (dpbuf[u, b] - dsum_ref[b] * inv)).astype(BF)
        added = dot(jnp.concatenate([dscore, prob.astype(BF)], axis=1), qdz[i])
        acc[u] += added.reshape(per, F, rows, PAIR)
        dqacc[i] += dot(kt[u], dscore)

    def red_copy(u, dc):
        return pltpu.make_async_remote_copy(
            src_ref=red_send.at[u, dc - 1], dst_ref=red_in.at[u, dc - 1],
            send_sem=red_ss.at[u * (fs - 1) + dc - 1], recv_sem=red_rs.at[u * (fs - 1) + dc - 1],
            device_id=(a0 * fs + lax.rem(c + dc, fs), w), device_id_type=MESH)

    def ship_part(u):
        for dc in range(1, fs):
            for gi in range(R):
                red_send[u, dc - 1, gi] = acc[u, :, lax.rem(c + dc, fs) + fs * gi].astype(BF)
            red_copy(u, dc).start()

    def fin_copy(t):
        dw = lax.div(t, R)
        aa, ww = lax.rem(a0 + lax.rem(t, R), R), behind(dw)
        return pltpu.make_async_remote_copy(
            src_ref=fin_send.at[lax.div(dw, per), aa, lax.rem(dw, per)], dst_ref=fin_in.at[head],
            send_sem=fin_ss.at[t], recv_sem=fin_rs.at[head],
            device_id=(aa * fs + c, ww), device_id_type=MESH)

    def ship_home(u):
        for dc in range(1, fs):
            red_copy(u, dc).wait_recv()
        for gi in range(R):
            whole = acc[u, :, c + fs * gi]
            for dc in range(1, fs):
                whole = whole + red_in[u, dc - 1, gi].astype(F32)
            fin_send[u, gi] = whole.astype(BF)
        if u == 0:
            fin_in[head] = fin_send[0, a0, 0]
        each(max(u * per * R, 1), (u + 1) * per * R, lambda t: fin_copy(t).start())

    def take_queries():
        each(1, R * W, lambda t: qd_arrival(t).wait_recv())
        wide = lax.broadcasted_iota(jnp.int32, (nq, PAIR), 1)
        tall = lax.broadcasted_iota(jnp.int32, (nq, PAIR), 0)
        both = qd_in[...].astype(F32).reshape(nq, PAIR)
        mark = jnp.zeros((nq, PAIR), F32)
        for gi in range(R):
            mine = (tall >= gi * seq) & (tall < (gi + 1) * seq)
            mark = jnp.where(mine & (wide >= DH + SPLITS * gi) & (wide < DH + SPLITS * (gi + 1)), 1.0, mark)
        scaled = both * scale
        qaug[...] = jnp.where(wide < DH, scaled, mark).astype(BF)
        xraw[...] = both.astype(BF)
        qdz[:, :QC] = jnp.where(wide < DH, scaled, 0.0).astype(BF).reshape(n_chunks, QC, PAIR)
        qdz[:, QC:] = jnp.where(wide >= DH, both, 0.0).astype(BF).reshape(n_chunks, QC, PAIR)

    take_queries()
    if inline:
        each(0, n_chunks, begin)
        direct(0)
        for u in range(n_units):
            settle(u)
            forth(u, 0, 0)
            if u + 1 < n_units:
                direct(u + 1)
            each(1, n_chunks, lambda i: forth(u, i, i))
        for u in range(n_units):
            each(0, n_chunks, lambda i: back(u, i, i))
            ship_part(u)
            if u:
                ship_home(u - 1)
    else:
        for u in range(n_units):
            direct(u)
        for u in range(n_units):
            settle(u)

        def block(i):
            begin(0)
            each(0, n_units, lambda u: forth(u, i, 0))
            each(0, n_units, lambda u: back(u, i, 0))

        each(0, n_chunks, block)
        for u in range(n_units):
            ship_part(u)
        for u in range(n_units - 1):
            ship_home(u)

    def dq_copy(t):
        aa, ww = lax.rem(a0 + lax.rem(t, R), R), behind(lax.div(t, R))
        return pltpu.make_async_remote_copy(
            src_ref=dq_send.at[aa, ww], dst_ref=dq_in.at[head],
            send_sem=dq_ss.at[t], recv_sem=dq_rs.at[head],
            device_id=(aa * fs + c, ww), device_id_type=MESH)

    for i in range(n_chunks):
        dqs[i * QC:(i + 1) * QC] = jnp.concatenate([dqacc[i], jnp.zeros((DH, QC), F32)], axis=0).T
    for gi in range(R):
        for ww in range(W):
            base = gi * seq + ww * rows
            dq_send[gi, ww] = jnp.concatenate(
                [dqs[base:base + half, :DH], dqs[base + rows - half:base + rows, :DH]], axis=1).astype(BF)
    dq_in[head] = dq_send[a0, w]
    each(1, R * W, lambda t: dq_copy(t).start())
    ship_home(n_units - 1)

    each(1, R * W, lambda t: head_arrival(t, dq_in, dq_ss, dq_rs).wait_recv())
    for j in range(width // PAIR):
        cols = slice(j * PAIR, (j + 1) * PAIR)
        sides = []
        for h in (2 * j, 2 * j + 1):
            got = dq_in[h].astype(F32)
            sides.append(jnp.concatenate([got[:, :DH], got[2 * half - rows:, DH:]], axis=0))
        dq_out[0, :, cols] = jnp.concatenate(sides, axis=1).astype(BF)

    each(1, R * W, lambda t: head_arrival(t, fin_in, fin_ss, fin_rs).wait_recv())
    for j in range(width // PAIR):
        cols = slice(j * PAIR, (j + 1) * PAIR)
        one, two = fin_in[2 * j], fin_in[2 * j + 1]
        dk_out[0, :, cols] = jnp.concatenate([one[:, :DH], two[:, :DH]], axis=1)
        dv_out[0, :, cols] = jnp.concatenate([one[:, DH:], two[:, DH:]], axis=1)

    each(1, hf * W, lambda t: kv_copy(t).wait_send())
    each(0, hf * W, lambda t: pass_on(f, t).wait_send())
    each(1, R * W, lambda t: qd_copy(t).wait_send())
    each(1, R * W, lambda t: dq_copy(t).wait_send())
    each(1, R * W, lambda t: fin_copy(t).wait_send())
    for u in range(n_units):
        for dc in range(1, fs):
            red_copy(u, dc).wait_send()


def local(F, W, queries, keys_in, values_in, grad_out, partners, registers):
    _, rows, width = queries.shape
    heads = width // DH
    R = heads // W
    fs = F // R
    seq = rows * W
    nq = R * seq
    half = ((rows + 1) // 2 + 7) // 8 * 8
    inline = F * seq * nq * 8 <= 24 * 2 ** 20
    QC = next(b for b in ((384, 256, 128) if inline else (128,)) if nq % b == 0)
    held = nq // QC if inline else 1
    per = next(n for n in range(W, 0, -1) if W % n == 0 and (n == 1 or n * F * rows <= UNIT))
    units = W // per
    unit = per * F * rows
    vm = lambda *shape: pltpu.VMEM(shape, BF)
    vf = lambda *shape: pltpu.VMEM(shape, F32)
    dma = lambda n: pltpu.SemaphoreType.DMA((n,))
    out = jax.ShapeDtypeStruct((1, rows, width), BF)
    return pl.pallas_call(
        functools.partial(kernel, F, W, R, QC, inline),
        out_shape=(out, out, out),
        in_specs=[pl.BlockSpec(memory_space=pltpu.SMEM)] * 2 + [pl.BlockSpec(memory_space=pltpu.VMEM)] * 4,
        out_specs=(pl.BlockSpec(memory_space=pltpu.VMEM),) * 3,
        scratch_shapes=[
            vm(heads, rows, PAIR), vm(heads, rows, PAIR),
            vm(F, W, rows, PAIR), vm(R, W, rows, PAIR),
            vm(units, unit, PAIR), vm(units, unit, PAIR), vm(units, DH, unit),
            vm(nq, PAIR), vm(nq, PAIR), vm(nq // QC, 2 * QC, PAIR),
            vf(units, held, unit, QC), vf(units, held, unit, QC), vf(units, per, F, rows, PAIR),
            vf(nq // QC, DH, QC), vf(nq, PAIR),
            vf(units, held, 1, QC), vf(held, 1, QC), vf(held, 1, QC), vf(held, 1, QC),
            vm(units, fs - 1, R, per, rows, PAIR), vm(units, fs - 1, R, per, rows, PAIR),
            vm(units, R, per, rows, PAIR), vm(heads, rows, PAIR),
            vm(R, W, half, PAIR), vm(heads, half, PAIR),
            dma(F // 2 * W), dma(F // 2 * W), dma(F * W), dma(R * W), dma(R * W),
            dma(units * (fs - 1)), dma(units * (fs - 1)), dma(R * W), dma(heads), dma(R * W), dma(heads),
        ],
        compiler_params=pltpu.CompilerParams(
            collective_id=0, has_side_effects=True, vmem_limit_bytes=60 * 2 ** 20),
    )(partners.T, registers, queries, keys_in, values_in, grad_out)


def solution(mesh):
    spec = P("frame", "within", None)
    return jax.shard_map(
        functools.partial(local, mesh.shape["frame"], mesh.shape["within"]),
        mesh=mesh,
        in_specs=(spec, spec, spec, spec, P(), P()),
        out_specs=(spec, spec, spec),
        check_vma=False,
    )
```

time: 56.2 us -> 53.1 us (0.945)
  Pallas kernels: 50.7 us -> 49 us
  local copies, waits for them, and re-layouts: 4.58 us -> 3.25 us
    pallas_call x1, Pallas kernels: 50.7 us -> 49 us  [local(): pl.pallas_call(functools.partial(kernel, F, W, R, QC, inline), out_shape=...]
    unnamed x8 -> x7, local copies, waits for them, and re-layouts: 4.58 us -> 3.25 us
where the time goes in v2:
time: 53.1 us; the launch traced here: 52.9 us
  Pallas kernels  49 us (92%)
  local copies, waits for them, and re-layouts  3.25 us (6%)
  between operations  0.65 us (1%)
    pallas_call x1, Pallas kernels, local(): pl.pallas_call(functools.partial(kernel, F, W, R, QC, inline), out_shape=...  49 us
    unnamed x7, local copies, waits for them, and re-layouts  3.25 us

profile of v2, /device:TPU:0, one launch (start us, length us, event | category | flops | bytes accessed | tf_op | source)
XLA Modules:
  0.0 52.9 jit_solution(14859089923648846643)
XLA Ops:
  0.6 49.0 %shard_map.85 = (bf16[1,72,1024]{2,1,0:T(8,128)(2,1)}, bf16[1,72,1024]{2,1,0:T(8,128)(2,1)}, bf16[1,72,1024]{2,1,0:T(8,128)(2,1)}) custom-call(s32[2,4]{1,0:T(2,128)} %bitcast.1, s32[4]{0:T(128)} %reg_ref.1, bf16[1,72,1024]{2,1,0:T(8,128)(2,1)} %q_ref.1, bf16[1,72,1024]{2,1,0:T(8,128)(2,1)} %k_ref.1, bf16[1,72,1024]{2,1,0:T(8,128)(2,1)} %v_ref.1, ...), custom_call_target="tpu_custom_call" | custom-call | tf_op jit(solution)/shard_map/pallas_call | solution.py:364
  49.7 0.0 copy-start.1
  49.7 1.6 %copy.12 = bf16[1,72,1024]{2,1,0:T(8,128)(2,1)} copy(bf16[1,72,1024]{2,1,0:T(8,128)(2,1)} %get-tuple-element.6) | data formatting | bytes 294912
  51.3 0.0 copy-done.1
  51.3 0.0 copy-start
  51.3 0.7 %copy.13 = bf16[1,72,1024]{2,1,0:T(8,128)(2,1)} copy(bf16[1,72,1024]{2,1,0:T(8,128)(2,1)S(1)} %copy-done.1) | data formatting | bytes 294912
  52.0 0.3 copy-done
  52.3 0.7 %copy.14 = bf16[1,72,1024]{2,1,0:T(8,128)(2,1)} copy(bf16[1,72,1024]{2,1,0:T(8,128)(2,1)S(1)} %copy-done) | data formatting | bytes 294912
Async XLA Ops:
  49.7 1.6 %copy-start.1 = (bf16[1,72,1024]{2,1,0:T(8,128)(2,1)S(1)}, bf16[1,72,1024]{2,1,0:T(8,128)(2,1)}, u32[]{:S(2)}) copy-start(bf16[1,72,1024]{2,1,0:T(8,128)(2,1)} %get-tuple-element.7) | copy-start | bytes 442372
  51.3 1.0 %copy-start = (bf16[1,72,1024]{2,1,0:T(8,128)(2,1)S(1)}, bf16[1,72,1024]{2,1,0:T(8,128)(2,1)}, u32[]{:S(2)}) copy-start(bf16[1,72,1024]{2,1,0:T(8,128)(2,1)} %get-tuple-element.8) | copy-start | bytes 442372

commit v3 on v2

--- a/solution.py
+++ b/solution.py
@@ -43,10 +43,10 @@
     lax.fori_loop(lo, hi, step, 0)
 
 
-def kernel(F, W, R, QC, inline, part_ref, reg_ref, q_ref, k_ref, v_ref, d_ref, dq_out, dk_out, dv_out,
+def kernel(F, W, R, QC, inline, part_ref, reg_ref, q_ref, k_ref, v_ref, d_ref, dq_in, fin_in,
            kv_send, qd_send, kv_in, qd_in, kaug, vz, kt, qaug, xraw, qdz, sbuf, dpbuf, acc, dqacc, dqs,
            tops, top_ref, total_ref, dsum_ref,
-           red_send, red_in, fin_send, fin_in, dq_send, dq_in,
+           red_send, red_in, fin_send, dq_send, own_sem,
            kv_ss, fw_ss, kv_rs, qd_ss, qd_rs, red_ss, red_rs, fin_ss, fin_rs, dq_ss, dq_rs):
     fs = F // R
     hf = F // 2
@@ -220,6 +220,9 @@
         acc[u] += added.reshape(per, F, rows, PAIR)
         dqacc[i] += dot(kt[u], dscore)
 
+    def own_copy(block, buffer, n):
+        return pltpu.make_async_copy(block, buffer.at[head], own_sem.at[n])
+
     def red_copy(u, dc):
         return pltpu.make_async_remote_copy(
             src_ref=red_send.at[u, dc - 1], dst_ref=red_in.at[u, dc - 1],
@@ -249,7 +252,7 @@
                 whole = whole + red_in[u, dc - 1, gi].astype(F32)
             fin_send[u, gi] = whole.astype(BF)
         if u == 0:
-            fin_in[head] = fin_send[0, a0, 0]
+            own_copy(fin_send.at[0, a0, 0], fin_in, 0).start()
         each(max(u * per * R, 1), (u + 1) * per * R, lambda t: fin_copy(t).start())
 
     def take_queries():
@@ -278,10 +281,11 @@
                 direct(u + 1)
             each(1, n_chunks, lambda i: forth(u, i, i))
         for u in range(n_units):
-            each(0, n_chunks, lambda i: back(u, i, i))
-            ship_part(u)
+            back(u, 0, 0)
             if u:
                 ship_home(u - 1)
+            each(1, n_chunks, lambda i: back(u, i, i))
+            ship_part(u)
     else:
         for u in range(n_units):
             direct(u)
@@ -313,11 +317,26 @@
             base = gi * seq + ww * rows
             dq_send[gi, ww] = jnp.concatenate(
                 [dqs[base:base + half, :DH], dqs[base + rows - half:base + rows, :DH]], axis=1).astype(BF)
-    dq_in[head] = dq_send[a0, w]
+    own_copy(dq_send.at[a0, w], dq_in, 1).start()
     each(1, R * W, lambda t: dq_copy(t).start())
     ship_home(n_units - 1)
 
     each(1, R * W, lambda t: head_arrival(t, dq_in, dq_ss, dq_rs).wait_recv())
+    each(1, R * W, lambda t: head_arrival(t, fin_in, fin_ss, fin_rs).wait_recv())
+    each(1, hf * W, lambda t: kv_copy(t).wait_send())
+    each(0, hf * W, lambda t: pass_on(f, t).wait_send())
+    each(1, R * W, lambda t: qd_copy(t).wait_send())
+    own_copy(fin_send.at[0, a0, 0], fin_in, 0).wait()
+    own_copy(dq_send.at[a0, w], dq_in, 1).wait()
+    each(1, R * W, lambda t: dq_copy(t).wait_send())
+    each(1, R * W, lambda t: fin_copy(t).wait_send())
+    for u in range(n_units):
+        for dc in range(1, fs):
+            red_copy(u, dc).wait_send()
+
+
+def tokens_again(dq_in, fin_in, dq_out, dk_out, dv_out):
+    half, rows, width = dq_in.shape[1], dq_out.shape[1], dq_out.shape[2]
     for j in range(width // PAIR):
         cols = slice(j * PAIR, (j + 1) * PAIR)
         sides = []
@@ -326,21 +345,11 @@
             sides.append(jnp.concatenate([got[:, :DH], got[2 * half - rows:, DH:]], axis=0))
         dq_out[0, :, cols] = jnp.concatenate(sides, axis=1).astype(BF)
 
-    each(1, R * W, lambda t: head_arrival(t, fin_in, fin_ss, fin_rs).wait_recv())
     for j in range(width // PAIR):
         cols = slice(j * PAIR, (j + 1) * PAIR)
         one, two = fin_in[2 * j], fin_in[2 * j + 1]
         dk_out[0, :, cols] = jnp.concatenate([one[:, :DH], two[:, :DH]], axis=1)
         dv_out[0, :, cols] = jnp.concatenate([one[:, DH:], two[:, DH:]], axis=1)
-
-    each(1, hf * W, lambda t: kv_copy(t).wait_send())
-    each(0, hf * W, lambda t: pass_on(f, t).wait_send())
-    each(1, R * W, lambda t: qd_copy(t).wait_send())
-    each(1, R * W, lambda t: dq_copy(t).wait_send())
-    each(1, R * W, lambda t: fin_copy(t).wait_send())
-    for u in range(n_units):
-        for dc in range(1, fs):
-            red_copy(u, dc).wait_send()
 
 
 def local(F, W, queries, keys_in, values_in, grad_out, partners, registers):
@@ -352,7 +361,7 @@
     nq = R * seq
     half = ((rows + 1) // 2 + 7) // 8 * 8
     inline = F * seq * nq * 8 <= 24 * 2 ** 20
-    QC = next(b for b in ((384, 256, 128) if inline else (128,)) if nq % b == 0)
+    QC = next(b for b in ((576, 384, 128) if inline else (128,)) if nq % b == 0)
     held = nq // QC if inline else 1
     per = next(n for n in range(W, 0, -1) if W % n == 0 and (n == 1 or n * F * rows <= UNIT))
     units = W // per
@@ -361,11 +370,11 @@
     vf = lambda *shape: pltpu.VMEM(shape, F32)
     dma = lambda n: pltpu.SemaphoreType.DMA((n,))
     out = jax.ShapeDtypeStruct((1, rows, width), BF)
-    return pl.pallas_call(
+    dq_heads, kv_heads = pl.pallas_call(
         functools.partial(kernel, F, W, R, QC, inline),
-        out_shape=(out, out, out),
+        out_shape=(jax.ShapeDtypeStruct((heads, half, PAIR), BF), jax.ShapeDtypeStruct((heads, rows, PAIR), BF)),
         in_specs=[pl.BlockSpec(memory_space=pltpu.SMEM)] * 2 + [pl.BlockSpec(memory_space=pltpu.VMEM)] * 4,
-        out_specs=(pl.BlockSpec(memory_space=pltpu.VMEM),) * 3,
+        out_specs=(pl.BlockSpec(memory_space=pl.ANY),) * 2,
         scratch_shapes=[
             vm(heads, rows, PAIR), vm(heads, rows, PAIR),
             vm(F, W, rows, PAIR), vm(R, W, rows, PAIR),
@@ -375,14 +384,19 @@
             vf(nq // QC, DH, QC), vf(nq, PAIR),
             vf(units, held, 1, QC), vf(held, 1, QC), vf(held, 1, QC), vf(held, 1, QC),
             vm(units, fs - 1, R, per, rows, PAIR), vm(units, fs - 1, R, per, rows, PAIR),
-            vm(units, R, per, rows, PAIR), vm(heads, rows, PAIR),
-            vm(R, W, half, PAIR), vm(heads, half, PAIR),
+            vm(units, R, per, rows, PAIR), vm(R, W, half, PAIR), dma(2),
             dma(F // 2 * W), dma(F // 2 * W), dma(F * W), dma(R * W), dma(R * W),
             dma(units * (fs - 1)), dma(units * (fs - 1)), dma(R * W), dma(heads), dma(R * W), dma(heads),
         ],
         compiler_params=pltpu.CompilerParams(
             collective_id=0, has_side_effects=True, vmem_limit_bytes=60 * 2 ** 20),
     )(partners.T, registers, queries, keys_in, values_in, grad_out)
+    return pl.pallas_call(
+        tokens_again,
+        out_shape=(out, out, out),
+        in_specs=[pl.BlockSpec(memory_space=pltpu.VMEM)] * 2,
+        out_specs=(pl.BlockSpec(memory_space=pltpu.VMEM),) * 3,
+    )(dq_heads, kv_heads)
 
 
 def solution(mesh):

time: 53.1 us -> 50.7 us (0.955)
  local copies, waits for them, and re-layouts: 3.25 us -> 0 us
  Pallas kernels: 49 us -> 49.9 us
    unnamed x7 -> x0, local copies, waits for them, and re-layouts: 3.25 us -> none
    pallas_call x0 -> x1, Pallas kernels: none -> 1.99 us  [local(): pl.pallas_call(tokens_again, out_shape=(out, out, out), in_specs=[pl.Bloc...]
    pallas_call x1, Pallas kernels: 49 us -> 47.9 us  [local(): pl.pallas_call(functools.partial(kernel, F, W, R, QC, inline), out_shape=...]
where the time goes in v3:
time: 50.7 us; the launch traced here: 50.5 us
  Pallas kernels  49.9 us (98%)
  between operations  0.64 us (1%)
    pallas_call x1, Pallas kernels, local(): pl.pallas_call(functools.partial(kernel, F, W, R, QC, inline), out_shape=...  47.9 us
    pallas_call x1, Pallas kernels, local(): pl.pallas_call(tokens_again, out_shape=(out, out, out), in_specs=[pl.Bloc...  1.99 us

profile of v3, /device:TPU:0, one launch (start us, length us, event | category | flops | bytes accessed | tf_op | source)
XLA Modules:
  0.0 50.5 jit_solution(2906190576650278622)
XLA Ops:
  0.6 47.9 %shard_map.85 = (bf16[16,40,128]{2,1,0:T(8,128)(2,1)}, bf16[16,72,128]{2,1,0:T(8,128)(2,1)}) custom-call(s32[2,4]{1,0:T(2,128)} %bitcast.1, s32[4]{0:T(128)} %reg_ref.1, bf16[1,72,1024]{2,1,0:T(8,128)(2,1)} %q_ref.1, bf16[1,72,1024]{2,1,0:T(8,128)(2,1)} %k_ref.1, bf16[1,72,1024]{2,1,0:T(8,128)(2,1)} %v_ref.1, bf16[1,72,1024]{2,1,0:T(8,128)(2,1)} %d_ref.1), custom_call_target="tpu_custom_call" | custom-call | tf_op jit(solution)/shard_map/pallas_call | solution.py:373
  48.5 2.0 %shard_map.86 = (bf16[1,72,1024]{2,1,0:T(8,128)(2,1)}, bf16[1,72,1024]{2,1,0:T(8,128)(2,1)}, bf16[1,72,1024]{2,1,0:T(8,128)(2,1)}) custom-call(bf16[16,40,128]{2,1,0:T(8,128)(2,1)} %get-tuple-element.5.dq_in, bf16[16,72,128]{2,1,0:T(8,128)(2,1)} %get-tuple-element.6.fin_in), custom_call_target="tpu_custom_call" | custom-call | tf_op jit(solution)/shard_map/pallas_call | solution.py:394

commit v4 on v3

--- a/solution.py
+++ b/solution.py
@@ -70,10 +70,10 @@
     barrier = pltpu.get_barrier_semaphore()
 
     def ahead(dw):
+        return lax.rem(w + W - dw, W)
+
+    def behind(dw):
         return lax.rem(w + dw, W)
-
-    def behind(dw):
-        return lax.rem(w + W - dw, W)
 
     def greet(t):
         pl.semaphore_signal(barrier, inc=1, device_id=(lax.rem(f + 2 * lax.rem(t, hf), F), ahead(lax.div(t, hf))),

time: 50.7 us -> 48.1 us (0.949)
  Pallas kernels: 49.9 us -> 47.3 us
    pallas_call x1, Pallas kernels: 47.9 us -> 45.3 us  [local(): pl.pallas_call(functools.partial(kernel, F, W, R, QC, inline), out_shape=...]
where the time goes in v4:
time: 48.1 us; the launch traced here: 47.9 us
  Pallas kernels  47.3 us (98%)
  between operations  0.64 us (1%)
    pallas_call x1, Pallas kernels, local(): pl.pallas_call(functools.partial(kernel, F, W, R, QC, inline), out_shape=...  45.3 us
    pallas_call x1, Pallas kernels, local(): pl.pallas_call(tokens_again, out_shape=(out, out, out), in_specs=[pl.Bloc...  1.99 us

profile of v4, /device:TPU:0, one launch (start us, length us, event | category | flops | bytes accessed | tf_op | source)
XLA Modules:
  0.0 47.9 jit_solution(14455702739967276086)
XLA Ops:
  0.6 45.3 %shard_map.85 = (bf16[16,40,128]{2,1,0:T(8,128)(2,1)}, bf16[16,72,128]{2,1,0:T(8,128)(2,1)}) custom-call(s32[2,4]{1,0:T(2,128)} %bitcast.1, s32[4]{0:T(128)} %reg_ref.1, bf16[1,72,1024]{2,1,0:T(8,128)(2,1)} %q_ref.1, bf16[1,72,1024]{2,1,0:T(8,128)(2,1)} %k_ref.1, bf16[1,72,1024]{2,1,0:T(8,128)(2,1)} %v_ref.1, bf16[1,72,1024]{2,1,0:T(8,128)(2,1)} %d_ref.1), custom_call_target="tpu_custom_call" | custom-call | tf_op jit(solution)/shard_map/pallas_call | solution.py:373
  45.9 2.0 %shard_map.86 = (bf16[1,72,1024]{2,1,0:T(8,128)(2,1)}, bf16[1,72,1024]{2,1,0:T(8,128)(2,1)}, bf16[1,72,1024]{2,1,0:T(8,128)(2,1)}) custom-call(bf16[16,40,128]{2,1,0:T(8,128)(2,1)} %get-tuple-element.5.dq_in, bf16[16,72,128]{2,1,0:T(8,128)(2,1)} %get-tuple-element.6.fin_in), custom_call_target="tpu_custom_call" | custom-call | tf_op jit(solution)/shard_map/pallas_call | solution.py:394
